TPU v7x, 32 devices: a whole 2x2x4 slice. The times are simulated.
32 devices in a mesh: groups: 2 (over y), req: 2 (over core), ctx: 8 (over z, x).
Axes of the slice: x: 2, y: 2, z: 4, core: 2. Of those that a mesh axis runs over, the one named last changes fastest.
Arguments:
- queries: bfloat16 [4, 1024, 4096], P(('groups', 'req'), 'ctx'), parts along dimension 0, may hold values from -6 to 6
- keys: bfloat16 [4, 1024, 512], P(('groups', 'req'), 'ctx'), parts along dimension 0, may hold values from -6 to 6
- values: bfloat16 [4, 1024, 512], P(('groups', 'req'), 'ctx'), parts along dimension 0, may hold values from -6 to 6
- cache_keys: bfloat16 [16, 256, 512], P(('groups', 'ctx')), parts along dimension 0, may hold values from -6 to 6
- cache_values: bfloat16 [16, 256, 512], P(('groups', 'ctx')), parts along dimension 0, may hold values from -6 to 6
- doc_lengths: int32 [4], P('groups'), parts along dimension 0, may hold values from 32 to 256, as said below
- doc_owners: int32 [4], P('groups'), parts along dimension 0, may hold values from 0 to 7, as said below
- block_offsets: int32 [4], P('groups'), parts along dimension 0, may hold values from 1 to 7
Outputs:
- attended: bfloat16 [4, 1024, 4096], P(('groups', 'req'), 'ctx'), parts along dimension 0
There are 2 independent parts, one for each index of `groups`. A program takes and returns all parts, laid end to end along the dimension named above; each array names one. Nothing has to cross between parts.
Inputs may be any that keep to these rules, and one draw needn't show every extreme that they name: `doc_lengths`: one document block has exactly 256 live rows. `doc_owners`: the owners of the two document blocks differ.
All inputs are finite; a program needn't handle non-finite values.
Results may differ from a plain program's by a relative error of at most 0.0065.
Values may be sent and summed in bfloat16 or wider, within the bound.
No kernel may reach another device: no remote copies, remote signals or barrier semaphores. Data moves between devices by JAX's collectives and lax.ppermute only.
A program may use at most 64 MiB of HBM per device.

v0:
```python
import math
import jax
import jax.numpy as jnp
from jax import lax
from jax.sharding import PartitionSpec as P

HD = 128
HOPS = 3
NEGATIVE = -1e30


def broadcast(block, axis, source):
    block = jnp.where(lax.axis_index(axis) == source, block, jnp.zeros_like(block))
    return lax.psum(block, axis)


def from_behind(value, axis, steps):
    count = lax.axis_size(axis)
    pairs = [(source, (source + steps) % count) for source in range(count)]
    return lax.ppermute(value, axis, pairs)


def merge_block(carried, query_rows, key_rows, value_rows, allowed):
    running, totals, summed = carried
    scores = jnp.einsum(
        "tid,sd->its", query_rows, key_rows, preferred_element_type=jnp.float32
    ) / math.sqrt(HD)
    scores = jnp.where(allowed[None], scores, NEGATIVE)
    highest = jnp.maximum(running, jnp.max(scores, axis=-1))
    weights = jnp.where(allowed[None], jnp.exp(scores - highest[..., None]), 0.0)
    shrink = jnp.exp(running - highest)
    totals = totals * shrink + jnp.sum(weights, axis=-1)
    summed = summed * shrink[..., None] + jnp.einsum(
        "its,sd->itd", weights.astype(jnp.bfloat16), value_rows, preferred_element_type=jnp.float32
    )
    return (highest, totals, summed)


def per_device(
    queries, keys, values, cache_keys, cache_values, doc_lengths, doc_owners, block_offsets
):
    cycle_size = lax.axis_size("ctx")
    position = lax.axis_index("ctx")
    request = lax.axis_index("req")
    tokens = queries.shape[1]
    kv_width = keys.shape[2]
    kv_heads = kv_width // HD
    group_size = queries.shape[2] // kv_width
    doc_rows = cache_keys.shape[1]
    offset = jnp.sum(jnp.where(jnp.arange(block_offsets.shape[0]) == request, block_offsets, 0))
    placed = (position - offset) % cycle_size
    inside = jnp.arange(tokens)
    resident = jnp.stack([keys[0], values[0]])
    blocks = [(resident, inside[None, :] <= inside[:, None])]
    cached = jnp.stack([cache_keys[0], cache_values[0]])
    doc_pairs = [broadcast(cached, "ctx", doc_owners[number]) for number in range(2)]
    for number in range(2):
        doc_live = jnp.broadcast_to(
            jnp.arange(doc_rows)[None, :] < doc_lengths[number], (tokens, doc_rows)
        )
        blocks.append((doc_pairs[number], doc_live))
    moving = resident
    for hop_count in range(1, HOPS + 1):
        moving = from_behind(moving, "ctx", 1)
        blocks.append((moving, jnp.broadcast_to(placed >= hop_count, (tokens, tokens))))
    query_heads = queries[0].reshape(tokens, kv_heads, group_size, HD)
    outputs = []
    for head_index in range(kv_heads):
        columns = slice(head_index * HD, (head_index + 1) * HD)
        query_rows = query_heads[:, head_index]
        carried = (
            jnp.full((group_size, tokens), NEGATIVE, jnp.float32),
            jnp.zeros((group_size, tokens), jnp.float32),
            jnp.zeros((group_size, tokens, HD), jnp.float32),
        )
        for paired, allowed in blocks:
            carried = merge_block(
                carried, query_rows, paired[0][:, columns], paired[1][:, columns], allowed
            )
        outputs.append(jnp.transpose(carried[2] / carried[1][..., None], (1, 0, 2)))
    attended = jnp.stack(outputs, axis=1).reshape(tokens, kv_heads * group_size * HD)
    return attended.astype(jnp.bfloat16)[None]


def solution(mesh):
    return jax.shard_map(
        per_device,
        mesh=mesh,
        in_specs=(
            P(("groups", "req"), "ctx", None),
            P(("groups", "req"), "ctx", None),
            P(("groups", "req"), "ctx", None),
            P(("groups", "ctx"), None, None),
            P(("groups", "ctx"), None, None),
            P("groups"),
            P("groups"),
            P("groups"),
        ),
        out_specs=P(("groups", "req"), "ctx", None),
        check_vma=False,
    )
```

profile of v0, /device:TPU:0, one launch (start us, length us, event | category | flops | bytes accessed | tf_op | source)
XLA Modules:
  0.0 129.9 jit_solution(4399630337771953146)
XLA Ops:
  6.5 1.0 pad_maximum_fusion.1
  7.6 3.0 %collective-permute-start = (bf16[2,128,512]{2,1,0:T(8,128)(2,1)S(1)}, bf16[2,128,512]{2,1,0:T(8,128)(2,1)S(1)}, u32[]{:S(2)}, u32[]{:S(2)}) collective-permute-start(bf16[2,128,512]{2,1,0:T(8,128)(2,1)S(1)} %pad_maximum_fusion.1), channel_id=1, source_target_pairs={{0,1},{1,2},{2,3},{3,4},{4,5},{5,6},{6,7},{7,0},{8,9},{9,10},{10,1... | collective-permute-start | bytes 786440 | tf_op jit(solution)/shard_map/ppermute | solution.py:20
  13.3 0.9 copy-done.16
  14.3 1.1 broadcast_select_fusion.1
  16.8 1.6 %fusion.350 = (f32[8,128]{1,0:T(8,128)}, f32[8,128,128]{1,2,0:T(8,128)}) fusion(bf16[128,4,8,128]{0,3,2,1:T(8,128)(2,1)S(1)} %bitcast.900, bf16[128,512]{1,0:T(8,128)(2,1)S(1)} %bitcast.929, pred[128,128]{0,1:T(8,128)(4,1)S(1)} %iota_compare_fusion), kind=kOutput, calls=%fused_computation.530 | convolution fusion | flops 33946624 | bytes 839680 | tf_op jit(solution)/shard_map/tid,sd->its/dot_general | solution.py:25
  18.4 1.6 %fusion.344 = (f32[8,128]{1,0:T(8,128)}, f32[8,128,128]{1,2,0:T(8,128)}) fusion(bf16[128,4,8,128]{0,3,2,1:T(8,128)(2,1)S(1)} %bitcast.901, bf16[128,512]{1,0:T(8,128)(2,1)S(1)} %bitcast.930, pred[128,128]{0,1:T(8,128)(4,1)S(1)} %iota_compare_fusion), kind=kOutput, calls=%fused_computation.524 | convolution fusion | flops 33946624 | bytes 839680 | tf_op jit(solution)/shard_map/tid,sd->its/dot_general | solution.py:25
  20.0 1.6 %fusion.338 = (f32[8,128]{1,0:T(8,128)}, f32[8,128,128]{1,2,0:T(8,128)}) fusion(bf16[128,4,8,128]{0,3,2,1:T(8,128)(2,1)S(1)} %bitcast.902, bf16[128,512]{1,0:T(8,128)(2,1)S(1)} %bitcast.931, pred[128,128]{0,1:T(8,128)(4,1)S(1)} %iota_compare_fusion), kind=kOutput, calls=%fused_computation.518 | convolution fusion | flops 33946624 | bytes 839680 | tf_op jit(solution)/shard_map/tid,sd->its/dot_general | solution.py:25
  22.9 1.2 iota_compare_fusion.1
  24.8 1.2 iota_compare_fusion.2
  26.9 1.6 %fusion.332 = (f32[8,128]{1,0:T(8,128)}, f32[8,128,128]{1,2,0:T(8,128)}) fusion(bf16[128,4,8,128]{0,3,2,1:T(8,128)(2,1)S(1)} %bitcast.903, bf16[128,512]{1,0:T(8,128)(2,1)S(1)} %bitcast.932, pred[128,128]{0,1:T(8,128)(4,1)S(1)} %iota_compare_fusion), kind=kOutput, calls=%fused_computation.512 | convolution fusion | flops 33946624 | bytes 839680 | tf_op jit(solution)/shard_map/tid,sd->its/dot_general | solution.py:25
  28.5 0.8 fusion.347
  29.3 1.6 %fusion.341 = (f32[8,128]{1,0:T(8,128)}, f32[8,128,128]{1,2,0:T(8,128)}) fusion(bf16[128,4,8,128]{0,3,2,1:T(8,128)(2,1)S(1)} %bitcast.905, bf16[128,512]{1,0:T(8,128)(2,1)S(1)} %get-tuple-element.70, pred[]{:T(512)S(6)} %ge.9), kind=kOutput, calls=%fused_computation.521 | convolution fusion | flops 33946624 | bytes 823297 | tf_op jit(solution)/shard_map/tid,sd->its/dot_general | solution.py:25
  30.9 1.5 %collective-permute-start.1 = (bf16[2,128,512]{2,1,0:T(8,128)(2,1)S(1)}, bf16[2,128,512]{2,1,0:T(8,128)(2,1)S(1)}, u32[]{:S(2)}, u32[]{:S(2)}) collective-permute-start(bf16[2,128,512]{2,1,0:T(8,128)(2,1)S(1)} %collective-permute-done), channel_id=1, source_target_pairs={{0,1},{1,2},{2,3},{3,4},{4,5},{5,6},{6,7},{7,0},{8,9},{9,10},{10,1... | collective-permute-start | bytes 786440 | tf_op jit(solution)/shard_map/ppermute | solution.py:20
  32.5 1.6 %fusion.335 = (f32[8,128]{1,0:T(8,128)}, f32[8,128,128]{1,2,0:T(8,128)}) fusion(bf16[128,4,8,128]{0,3,2,1:T(8,128)(2,1)S(1)} %bitcast.906, bf16[128,512]{1,0:T(8,128)(2,1)S(1)} %get-tuple-element.70, pred[]{:T(512)S(6)} %ge.9), kind=kOutput, calls=%fused_computation.515 | convolution fusion | flops 33946624 | bytes 823297 | tf_op jit(solution)/shard_map/tid,sd->its/dot_general | solution.py:25
  34.1 0.8 fusion.329
  34.9 8.0 %collective-permute-done.1 = bf16[2,128,512]{2,1,0:T(8,128)(2,1)S(1)} collective-permute-done((bf16[2,128,512]{2,1,0:T(8,128)(2,1)S(1)}, bf16[2,128,512]{2,1,0:T(8,128)(2,1)S(1)}, u32[]{:S(2)}, u32[]{:S(2)}) %collective-permute-start.1) | collective-permute-done | bytes 262176 | tf_op jit(solution)/shard_map/ppermute | solution.py:20
  43.0 0.8 fusion.346
  43.8 1.6 %fusion.340 = (f32[8,128]{1,0:T(8,128)}, f32[8,128,128]{1,2,0:T(8,128)}) fusion(bf16[128,4,8,128]{0,3,2,1:T(8,128)(2,1)S(1)} %bitcast.909, bf16[128,512]{1,0:T(8,128)(2,1)S(1)} %get-tuple-element.68, pred[]{:T(512)S(6)} %ge.10), kind=kOutput, calls=%fused_computation.520 | convolution fusion | flops 33946624 | bytes 823297 | tf_op jit(solution)/shard_map/tid,sd->its/dot_general | solution.py:25
  45.4 1.6 %fusion.334 = (f32[8,128]{1,0:T(8,128)}, f32[8,128,128]{1,2,0:T(8,128)}) fusion(bf16[128,4,8,128]{0,3,2,1:T(8,128)(2,1)S(1)} %bitcast.910, bf16[128,512]{1,0:T(8,128)(2,1)S(1)} %get-tuple-element.68, pred[]{:T(512)S(6)} %ge.10), kind=kOutput, calls=%fused_computation.514 | convolution fusion | flops 33946624 | bytes 823297 | tf_op jit(solution)/shard_map/tid,sd->its/dot_general | solution.py:25
  47.0 0.8 fusion.328
  47.9 10.0 %collective-permute-done.2 = bf16[2,128,512]{2,1,0:T(8,128)(2,1)S(1)} collective-permute-done((bf16[2,128,512]{2,1,0:T(8,128)(2,1)S(1)}, bf16[2,128,512]{2,1,0:T(8,128)(2,1)S(1)}, u32[]{:S(2)}, u32[]{:S(2)}) %collective-permute-start.2) | collective-permute-done | bytes 262176 | tf_op jit(solution)/shard_map/ppermute | solution.py:20
  58.5 1.6 %fusion.345 = (f32[8,128]{1,0:T(8,128)}, f32[8,128,128]{1,2,0:T(8,128)}) fusion(bf16[128,4,8,128]{0,3,2,1:T(8,128)(2,1)S(1)} %bitcast.912, bf16[128,512]{1,0:T(8,128)(2,1)S(1)} %get-tuple-element.66, pred[]{:T(512)S(6)} %ge.11), kind=kOutput, calls=%fused_computation.525 | convolution fusion | flops 33946624 | bytes 823297 | tf_op jit(solution)/shard_map/tid,sd->its/dot_general | solution.py:25
  60.2 1.6 %fusion.339 = (f32[8,128]{1,0:T(8,128)}, f32[8,128,128]{1,2,0:T(8,128)}) fusion(bf16[128,4,8,128]{0,3,2,1:T(8,128)(2,1)S(1)} %bitcast.913, bf16[128,512]{1,0:T(8,128)(2,1)S(1)} %get-tuple-element.66, pred[]{:T(512)S(6)} %ge.11), kind=kOutput, calls=%fused_computation.519 | convolution fusion | flops 33946624 | bytes 823297 | tf_op jit(solution)/shard_map/tid,sd->its/dot_general | solution.py:25
  61.8 1.6 %fusion.333 = (f32[8,128]{1,0:T(8,128)}, f32[8,128,128]{1,2,0:T(8,128)}) fusion(bf16[128,4,8,128]{0,3,2,1:T(8,128)(2,1)S(1)} %bitcast.914, bf16[128,512]{1,0:T(8,128)(2,1)S(1)} %get-tuple-element.66, pred[]{:T(512)S(6)} %ge.11), kind=kOutput, calls=%fused_computation.513 | convolution fusion | flops 33946624 | bytes 823297 | tf_op jit(solution)/shard_map/tid,sd->its/dot_general | solution.py:25
  63.4 1.6 %fusion.327 = (f32[8,128]{1,0:T(8,128)}, f32[8,128,128]{1,2,0:T(8,128)}) fusion(bf16[128,4,8,128]{0,3,2,1:T(8,128)(2,1)S(1)} %bitcast.915, bf16[128,512]{1,0:T(8,128)(2,1)S(1)} %get-tuple-element.66, pred[]{:T(512)S(6)} %ge.11), kind=kOutput, calls=%fused_computation.507 | convolution fusion | flops 33946624 | bytes 823297 | tf_op jit(solution)/shard_map/tid,sd->its/dot_general | solution.py:25
  65.0 32.8 %all-reduce.3.cloned.1.call-done = (bf16[2,256,512]{2,1,0:T(8,128)(2,1)}, bf16[2,256,512]{2,1,0:T(8,128)(2,1)}) async-done(((bf16[2,256,512]{2,1,0:T(8,128)(2,1)}, bf16[2,256,512]{2,1,0:T(8,128)(2,1)}), (bf16[2,256,512]{2,1,0:T(8,128)(2,1)}, bf16[2,256,512]{2,1,0:T(8,128)(2,1)})) %all-reduce.3.cloned.1.call-update) | async-done | bytes 1048592 | tf_op jit(solution)/shard_map/psum | solution.py:14
  97.8 1.3 slice_bitcast_fusion.3
  106.7 0.9 fusion.106
  108.1 1.0 copy-done.3
  111.9 0.8 fusion.104
  119.2 0.8 copy-done.8
  121.7 1.3 %copy.105 = bf16[1,128,4096]{2,1,0:T(8,128)(2,1)} copy(bf16[1,128,4096]{1,2,0:T(8,128)(2,1)S(1)} %bitcast.924) | data formatting | bytes 2097152 | tf_op jit(solution)/shard_map/convert_element_type | solution.py:82
  (144 shorter events, 24.2 us)
Async XLA Ops:
  6.5 6.7 %copy-start.15 = (bf16[1,256,512]{2,1,0:T(8,128)(2,1)S(1)}, bf16[1,256,512]{2,1,0:T(8,128)(2,1)}, u32[]{:S(2)}) copy-start(bf16[1,256,512]{2,1,0:T(8,128)(2,1)} %param.11) | copy-start | bytes 786436
  6.5 91.3 %all-reduce.3.cloned.1.call-start = ((), (), s32[]{:S(2)}) async-start(), calls=%async_computation | async-start | bytes 2097152 | tf_op jit(solution)/shard_map/psum | solution.py:14
  7.6 20.9 %collective-permute-start = (bf16[2,128,512]{2,1,0:T(8,128)(2,1)S(1)}, bf16[2,128,512]{2,1,0:T(8,128)(2,1)S(1)}, u32[]{:S(2)}, u32[]{:S(2)}) collective-permute-start(bf16[2,128,512]{2,1,0:T(8,128)(2,1)S(1)} %pad_maximum_fusion.1), channel_id=1, source_target_pairs={{0,1},{1,2},{2,3},{3,4},{4,5},{5,6},{6,7},{7,0},{8,9},{9,10},{10,1... | collective-permute-start | bytes 786440 | tf_op jit(solution)/shard_map/ppermute | solution.py:20
  13.3 1.0 copy-start.16
  14.2 1.6 %copy-start.12 = (bf16[1,128,4096]{2,1,0:T(8,128)(2,1)S(1)}, bf16[1,128,4096]{2,1,0:T(8,128)(2,1)}, u32[]{:S(2)}) copy-start(bf16[1,128,4096]{2,1,0:T(8,128)(2,1)} %param.8) | copy-start | bytes 3145732
  15.8 0.9 copy-start.13
  20.0 6.7 %copy-start.14 = (bf16[1,128,512]{2,1,0:T(8,128)(2,1)S(1)}, bf16[1,128,512]{2,1,0:T(8,128)(2,1)}, u32[]{:S(2)}) copy-start(bf16[1,128,512]{2,1,0:T(8,128)(2,1)} %param.10) | copy-start | bytes 393220
  22.9 1.2 copy-start.38
  30.9 12.0 %collective-permute-start.1 = (bf16[2,128,512]{2,1,0:T(8,128)(2,1)S(1)}, bf16[2,128,512]{2,1,0:T(8,128)(2,1)S(1)}, u32[]{:S(2)}, u32[]{:S(2)}) collective-permute-start(bf16[2,128,512]{2,1,0:T(8,128)(2,1)S(1)} %collective-permute-done), channel_id=1, source_target_pairs={{0,1},{1,2},{2,3},{3,4},{4,5},{5,6},{6,7},{7,0},{8,9},{9,10},{10,1... | collective-permute-start | bytes 786440 | tf_op jit(solution)/shard_map/ppermute | solution.py:20
  45.4 12.5 %collective-permute-start.2 = (bf16[2,128,512]{2,1,0:T(8,128)(2,1)S(1)}, bf16[2,128,512]{2,1,0:T(8,128)(2,1)S(1)}, u32[]{:S(2)}, u32[]{:S(2)}) collective-permute-start(bf16[2,128,512]{2,1,0:T(8,128)(2,1)S(1)} %collective-permute-done.1), channel_id=1, source_target_pairs={{0,1},{1,2},{2,3},{3,4},{4,5},{5,6},{6,7},{7,0},{8,9},{9,10},{10,1... | collective-permute-start | bytes 786440 | tf_op jit(solution)/shard_map/ppermute | solution.py:20
  102.5 0.7 copy-start.35
  102.8 0.7 copy-start.32
  103.5 0.7 copy-start.31
  103.5 0.7 copy-start.33
  103.9 0.7 copy-start.26
  105.0 0.7 copy-start.25
  105.0 0.7 copy-start.20
  105.7 0.7 copy-start.24
  106.0 0.7 copy-start.21
  106.7 1.3 copy-start.11
  107.6 1.8 %copy-start.10 = (f32[8,128,128]{1,2,0:T(8,128)S(1)}, f32[8,128,128]{1,2,0:T(8,128)}, u32[]{:S(2)}) copy-start(f32[8,128,128]{1,2,0:T(8,128)} %get-tuple-element.112) | copy-start | bytes 1572868
  107.6 3.0 %copy-start.6 = (f32[8,128,128]{1,2,0:T(8,128)S(1)}, f32[8,128,128]{1,2,0:T(8,128)}, u32[]{:S(2)}) copy-start(f32[8,128,128]{1,2,0:T(8,128)} %get-tuple-element.122) | copy-start | bytes 1572868
  107.6 3.0 %copy-start.7 = (f32[8,128,128]{1,2,0:T(8,128)S(1)}, f32[8,128,128]{1,2,0:T(8,128)}, u32[]{:S(2)}) copy-start(f32[8,128,128]{1,2,0:T(8,128)} %get-tuple-element.110) | copy-start | bytes 1572868
  108.0 1.1 copy-start.3
  108.0 1.3 copy-start.2
  109.3 1.0 copy-start.1
  109.4 1.1 copy-start
  110.3 1.0 copy-start.4
  110.3 1.2 copy-start.5
  114.9 0.9 copy-start.17
  116.1 1.0 copy-start.9
  118.9 1.0 copy-start.8
  (11 other events, 7.3 us)
Sparse Core Ops, SparseCore 0:
  15.5 82.2 all-reduce.2
where the time goes:
time: 131 us; the launch traced here: 130 us
  waiting for transfers between devices  50.9 us (39%)
  matrix products  32.1 us (25%)
  local copies, waits for them, and re-layouts  17.4 us (13%)
  between operations  16.1 us (12%)
  other arithmetic  8.85 us (7%)
  starting transfers between devices  4.57 us (3%)
    psum x1, waiting for transfers between devices, broadcast(): return lax.psum(block, axis)  32.8 us
    dot_general x24, matrix products, merge_block(): jnp.einsum('tid,sd->its', query_rows, key_rows, preferred_element_type=jn...  25.1 us
    ppermute x3, waiting for transfers between devices, from_behind(): return lax.ppermute(value, axis, pairs)  18.1 us
    unnamed x81, local copies, waits for them, and re-layouts  12.8 us
    dot_general x24, matrix products, merge_block(): jnp.einsum('its,sd->itd', weights.astype(jnp.bfloat16), value_rows, prefe...  7.01 us
    ppermute x3, starting transfers between devices, from_behind(): return lax.ppermute(value, axis, pairs)  4.57 us
    reduce_sum x15, other arithmetic, merge_block(): totals = totals * shrink + jnp.sum(weights, axis=-1)  3.35 us
  transfers between devices with their start and end apart: 4, of which 3 were waited for; matrix products, arithmetic and copies ran while one was open for 23% of the time, Pallas kernels for 0%

commit v1 on v0

--- a/solution.py
+++ b/solution.py
@@ -11,7 +11,7 @@
 
 def broadcast(block, axis, source):
     block = jnp.where(lax.axis_index(axis) == source, block, jnp.zeros_like(block))
-    return lax.psum(block, axis)
+    return jnp.sum(lax.all_gather(block, axis), axis=0)
 
 
 def from_behind(value, axis, steps):

time: 131 us -> 199 us (1.52)
  waiting for transfers between devices: 50.9 us -> 112 us
  local copies, waits for them, and re-layouts: 17.4 us -> 8.65 us
  matrix products: 32.1 us -> 40.2 us
  other arithmetic: 8.85 us -> 16.7 us
    all_gather x0 -> x2, waiting for transfers between devices: none -> 99 us  [broadcast(): return jnp.sum(lax.all_gather(block, axis), axis=0)]
    psum x1 -> x0, waiting for transfers between devices: 32.8 us -> none  [broadcast(): return lax.psum(block, axis)]
    unnamed x81 -> x92, local copies, waits for them, and re-layouts: 12.8 us -> 2.2 us
    dot_general x24, matrix products: 25.1 us -> 33.2 us  [merge_block(): jnp.einsum('tid,sd->its', query_rows, key_rows, preferred_element_type=jn...]
    reduce_sum x0 -> x2, other arithmetic: none -> 6.68 us  [broadcast(): return jnp.sum(lax.all_gather(block, axis), axis=0)]
    ppermute x3, waiting for transfers between devices: 18.1 us -> 12 us  [from_behind(): return lax.ppermute(value, axis, pairs)]
    reduce_sum x15 -> x8, other arithmetic: 3.35 us -> 4.11 us  [merge_block(): totals = totals * shrink + jnp.sum(weights, axis=-1)]
  transfers between devices with their start and end apart: 4 -> 5, of which waited for: 3 -> 4; matrix products, arithmetic and copies ran while one was open for 23% -> 20% of each run, Pallas kernels for 0% -> 0%
where the time goes in v1:
time: 199 us; the launch traced here: 198 us
  waiting for transfers between devices  112 us (56%)
  matrix products  40.2 us (20%)
  other arithmetic  16.7 us (8%)
  between operations  16.3 us (8%)
  local copies, waits for them, and re-layouts  8.65 us (4%)
  starting transfers between devices  4.64 us (2%)
    all_gather x2, waiting for transfers between devices, broadcast(): return jnp.sum(lax.all_gather(block, axis), axis=0)  99 us
    dot_general x24, matrix products, merge_block(): jnp.einsum('tid,sd->its', query_rows, key_rows, preferred_element_type=jn...  33.2 us
    ppermute x3, waiting for transfers between devices, from_behind(): return lax.ppermute(value, axis, pairs)  12 us
    dot_general x24, matrix products, merge_block(): jnp.einsum('its,sd->itd', weights.astype(jnp.bfloat16), value_rows, prefe...  7 us
    reduce_sum x2, other arithmetic, broadcast(): return jnp.sum(lax.all_gather(block, axis), axis=0)  6.68 us
    ppermute x3, starting transfers between devices, from_behind(): return lax.ppermute(value, axis, pairs)  4.57 us
    reduce_sum x8, other arithmetic, merge_block(): totals = totals * shrink + jnp.sum(weights, axis=-1)  4.11 us
  transfers between devices with their start and end apart: 5, of which 4 were waited for; matrix products, arithmetic and copies ran while one was open for 20% of the time, Pallas kernels for 0%

profile of v1, /device:TPU:0, one launch (start us, length us, event | category | flops | bytes accessed | tf_op | source)
XLA Modules:
  0.0 198.2 jit_solution(13344420917345412719)
XLA Ops:
  6.6 1.4 fusion.325
  9.3 2.1 %broadcast_select_fusion.1 = (bf16[1,2,256,512]{3,2,1,0:T(8,128)(2,1)}, bf16[1,2,256,512]{3,2,1,0:T(8,128)(2,1)}) fusion(pred[]{:T(512)S(6)} %eq.14, bf16[1,1,256,512]{3,2,1,0:T(8,128)(2,1)} %bitcast.935, bf16[1,1,256,512]{3,2,1,0:T(8,128)(2,1)} %bitcast.936, pred[]{:T(512)S(6)} %eq.15), kind=kLoop, calls=%fused_computation.219 | loop fusion | flops 786432 | bytes 1572866 | tf_op jit(solution)/shard_map/jit(_where)/select_n | solution.py:13
  13.2 3.0 %collective-permute-start = (bf16[2,128,512]{2,1,0:T(8,128)(2,1)S(1)}, bf16[2,128,512]{2,1,0:T(8,128)(2,1)S(1)}, u32[]{:S(2)}, u32[]{:S(2)}) collective-permute-start(bf16[2,128,512]{2,1,0:T(8,128)(2,1)S(1)} %pad_maximum_fusion.2), channel_id=1, source_target_pairs={{0,1},{1,2},{2,3},{3,4},{4,5},{5,6},{6,7},{7,0},{8,9},{9,10},{10,1... | collective-permute-start | bytes 786440 | tf_op jit(solution)/shard_map/ppermute | solution.py:20
  16.2 1.6 copy.106
  19.8 1.7 fusion.338
  21.4 1.7 fusion.344
  23.1 1.6 fusion.350
  24.7 1.3 iota_compare_fusion.2
  26.7 1.6 fusion.332
  28.3 1.5 collective-permute-start.1
  30.6 1.6 fusion.335
  32.2 1.7 fusion.341
  33.8 1.6 fusion.347
  35.4 1.6 fusion.329
  37.1 8.3 %collective-permute-done.1 = bf16[2,128,512]{2,1,0:T(8,128)(2,1)S(1)} collective-permute-done((bf16[2,128,512]{2,1,0:T(8,128)(2,1)S(1)}, bf16[2,128,512]{2,1,0:T(8,128)(2,1)S(1)}, u32[]{:S(2)}, u32[]{:S(2)}) %collective-permute-start.1) | collective-permute-done | bytes 262176 | tf_op jit(solution)/shard_map/ppermute | solution.py:20
  46.1 1.6 fusion.334
  47.7 1.6 fusion.340
  49.3 1.6 fusion.346
  50.9 1.6 fusion.328
  52.5 3.7 %collective-permute-done.2 = bf16[2,128,512]{2,1,0:T(8,128)(2,1)S(1)} collective-permute-done((bf16[2,128,512]{2,1,0:T(8,128)(2,1)S(1)}, bf16[2,128,512]{2,1,0:T(8,128)(2,1)S(1)}, u32[]{:S(2)}, u32[]{:S(2)}) %collective-permute-start.2) | collective-permute-done | bytes 262176 | tf_op jit(solution)/shard_map/ppermute | solution.py:20
  56.9 1.6 fusion.333
  58.5 1.6 fusion.339
  60.1 1.6 fusion.345
  61.7 1.6 fusion.327
  63.3 29.8 %all-gather.5.cloned.1.call-done = bf16[8,2,256,512]{3,2,1,0:T(8,128)(2,1)} async-done(((bf16[1,2,256,512]{3,2,1,0:T(8,128)(2,1)}), bf16[8,2,256,512]{3,2,1,0:T(8,128)(2,1)}) %all-gather.5.cloned.1.call-update) | async-done | bytes 4194320 | tf_op jit(solution)/shard_map/all_gather | solution.py:14
  93.1 3.0 %reduce_sum.298 = bf16[2,256,512]{2,1,0:T(8,128)(2,1)S(1)} reduce(bf16[8,2,256,512]{3,2,1,0:T(8,128)(2,1)} %all-gather.5.cloned.1.call-done, bf16[]{:T(256)} %constant.60.clone.1), dimensions={0}, to_apply=%region_3.4 | reduce | flops 1835008 | bytes 4718594 | tf_op jit(solution)/shard_map/reduce_sum | solution.py:14
  97.0 1.5 fusion.342
  98.5 69.1 %all-gather.3.cloned.1.call-done = bf16[8,2,256,512]{3,2,1,0:T(8,128)(2,1)} async-done(((bf16[1,2,256,512]{3,2,1,0:T(8,128)(2,1)}), bf16[8,2,256,512]{3,2,1,0:T(8,128)(2,1)}) %all-gather.3.cloned.1.call-update) | async-done | bytes 4194320 | tf_op jit(solution)/shard_map/all_gather | solution.py:14
  167.7 3.7 %reduce_sum.297 = bf16[2,256,512]{2,1,0:T(8,128)(2,1)} reduce(bf16[8,2,256,512]{3,2,1,0:T(8,128)(2,1)} %all-gather.3.cloned.1.call-done, bf16[]{:T(256)} %constant.60.clone.1), dimensions={0}, to_apply=%region_1.2 | reduce | flops 1835008 | bytes 4718594 | tf_op jit(solution)/shard_map/reduce_sum | solution.py:14
  176.4 1.2 fusion.330
  180.5 2.5 %fusion.104 = (f32[8,128]{1,0:T(8,128)S(1)}, f32[8,128]{1,0:T(8,128)S(1)}, f32[8,128]{1,0:T(8,128)S(1)}, f32[8,128]{1,0:T(8,128)S(1)}, f32[8,128]{1,0:T(8,128)S(...) fusion(f32[8,128,256]{1,2,0:T(8,128)S(1)} %get-tuple-element.106, ...), kind=kLoop, calls=%fused_computation.161 | loop fusion | flops 6283264 | bytes 8454656 | tf_op jit(solution)/shard_map/reduce_sum | solution.py:32
  190.1 1.3 copy.156
  (153 shorter events, 20.8 us)
Async XLA Ops:
  6.5 20.0 %copy-start.20 = (bf16[1,128,512]{2,1,0:T(8,128)(2,1)S(1)}, bf16[1,128,512]{2,1,0:T(8,128)(2,1)}, u32[]{:S(2)}) copy-start(bf16[1,128,512]{2,1,0:T(8,128)(2,1)} %param.10) | copy-start | bytes 393220
  6.5 13.2 %copy-start.17 = (bf16[1,128,512]{2,1,0:T(8,128)(2,1)S(1)}, bf16[1,128,512]{2,1,0:T(8,128)(2,1)}, u32[]{:S(2)}) copy-start(bf16[1,128,512]{2,1,0:T(8,128)(2,1)} %param.9) | copy-start | bytes 393220
  6.5 11.3 %copy-start.43 = (s32[2]{0:T(128)S(1)}, s32[2]{0:T(128)}, u32[]{:S(2)}) copy-start(s32[2]{0:T(128)} %param.13) | copy-start | bytes 28
  6.5 12.6 %copy-start.44 = (s32[2]{0:T(128)S(1)}, s32[2]{0:T(128)}, u32[]{:S(2)}) copy-start(s32[2]{0:T(128)} %param.15) | copy-start | bytes 28
  6.5 86.6 %all-gather.5.cloned.1.call-start = ((), (), s32[]{:S(2)}) async-start(), calls=%async_computation.1 | async-start | bytes 4718592 | tf_op jit(solution)/shard_map/all_gather | solution.py:14
  11.4 156.2 %all-gather.3.cloned.1.call-start = ((), (), s32[]{:S(2)}) async-start(), calls=%async_computation | async-start | bytes 4718592 | tf_op jit(solution)/shard_map/all_gather | solution.py:14
  13.2 15.1 %collective-permute-start = (bf16[2,128,512]{2,1,0:T(8,128)(2,1)S(1)}, bf16[2,128,512]{2,1,0:T(8,128)(2,1)S(1)}, u32[]{:S(2)}, u32[]{:S(2)}) collective-permute-start(bf16[2,128,512]{2,1,0:T(8,128)(2,1)S(1)} %pad_maximum_fusion.2), channel_id=1, source_target_pairs={{0,1},{1,2},{2,3},{3,4},{4,5},{5,6},{6,7},{7,0},{8,9},{9,10},{10,1... | collective-permute-start | bytes 786440 | tf_op jit(solution)/shard_map/ppermute | solution.py:20
  19.1 77.0 %copy-start.23 = (pred[256]{0:T(512)(128)(4,1)}, pred[256]{0:T(512)(128)(4,1)S(1)}, u32[]{:S(2)}) copy-start(pred[256]{0:T(512)(128)(4,1)S(1)} %iota_compare_fusion.1) | copy-start | bytes 772
  28.3 17.1 %collective-permute-start.1 = (bf16[2,128,512]{2,1,0:T(8,128)(2,1)S(1)}, bf16[2,128,512]{2,1,0:T(8,128)(2,1)S(1)}, u32[]{:S(2)}, u32[]{:S(2)}) collective-permute-start(bf16[2,128,512]{2,1,0:T(8,128)(2,1)S(1)} %collective-permute-done), channel_id=1, source_target_pairs={{0,1},{1,2},{2,3},{3,4},{4,5},{5,6},{6,7},{7,0},{8,9},{9,10},{10,1... | collective-permute-start | bytes 786440 | tf_op jit(solution)/shard_map/ppermute | solution.py:20
  45.4 10.8 %collective-permute-start.2 = (bf16[2,128,512]{2,1,0:T(8,128)(2,1)S(1)}, bf16[2,128,512]{2,1,0:T(8,128)(2,1)S(1)}, u32[]{:S(2)}, u32[]{:S(2)}) collective-permute-start(bf16[2,128,512]{2,1,0:T(8,128)(2,1)S(1)} %collective-permute-done.1), channel_id=1, source_target_pairs={{0,1},{1,2},{2,3},{3,4},{4,5},{5,6},{6,7},{7,0},{8,9},{9,10},{10,1... | collective-permute-start | bytes 786440 | tf_op jit(solution)/shard_map/ppermute | solution.py:20
  171.4 4.3 %copy-start.22 = (pred[256]{0:T(512)(128)(4,1)S(1)}, pred[256]{0:T(512)(128)(4,1)}, u32[]{:S(2)}) copy-start(pred[256]{0:T(512)(128)(4,1)} %iota_compare_fusion.2) | copy-start | bytes 772
  171.4 4.9 %copy-start.24 = (pred[256]{0:T(512)(128)(4,1)S(1)}, pred[256]{0:T(512)(128)(4,1)}, u32[]{:S(2)}) copy-start(pred[256]{0:T(512)(128)(4,1)} %copy-done.23) | copy-start | bytes 772
  172.5 5.2 %copy-start.34 = (f32[8,128]{1,0:T(8,128)S(1)}, f32[8,128]{1,0:T(8,128)}, u32[]{:S(2)}) copy-start(f32[8,128]{1,0:T(8,128)} %get-tuple-element.107) | copy-start | bytes 12292
  172.5 5.2 %copy-start.37 = (f32[8,128]{1,0:T(8,128)S(1)}, f32[8,128]{1,0:T(8,128)}, u32[]{:S(2)}) copy-start(f32[8,128]{1,0:T(8,128)} %get-tuple-element.101) | copy-start | bytes 12292
  172.5 5.2 %copy-start.39 = (f32[8,128]{1,0:T(8,128)S(1)}, f32[8,128]{1,0:T(8,128)}, u32[]{:S(2)}) copy-start(f32[8,128]{1,0:T(8,128)} %get-tuple-element.99) | copy-start | bytes 12292
  172.5 5.2 %copy-start.41 = (f32[8,128]{1,0:T(8,128)S(1)}, f32[8,128]{1,0:T(8,128)}, u32[]{:S(2)}) copy-start(f32[8,128]{1,0:T(8,128)} %get-tuple-element.97) | copy-start | bytes 12292
  172.5 5.2 %copy-start.42 = (f32[8,128]{1,0:T(8,128)S(1)}, f32[8,128]{1,0:T(8,128)}, u32[]{:S(2)}) copy-start(f32[8,128]{1,0:T(8,128)} %get-tuple-element.103) | copy-start | bytes 12292
  173.5 4.6 %copy-start.32 = (f32[8,128]{1,0:T(8,128)S(1)}, f32[8,128]{1,0:T(8,128)}, u32[]{:S(2)}) copy-start(f32[8,128]{1,0:T(8,128)} %get-tuple-element.119) | copy-start | bytes 12292
  173.5 4.6 %copy-start.35 = (f32[8,128]{1,0:T(8,128)S(1)}, f32[8,128]{1,0:T(8,128)}, u32[]{:S(2)}) copy-start(f32[8,128]{1,0:T(8,128)} %get-tuple-element.113) | copy-start | bytes 12292
  173.5 4.6 %copy-start.36 = (f32[8,128]{1,0:T(8,128)S(1)}, f32[8,128]{1,0:T(8,128)}, u32[]{:S(2)}) copy-start(f32[8,128]{1,0:T(8,128)} %get-tuple-element.111) | copy-start | bytes 12292
  173.5 4.6 %copy-start.38 = (f32[8,128]{1,0:T(8,128)S(1)}, f32[8,128]{1,0:T(8,128)}, u32[]{:S(2)}) copy-start(f32[8,128]{1,0:T(8,128)} %get-tuple-element.109) | copy-start | bytes 12292
  173.5 4.6 %copy-start.40 = (f32[8,128]{1,0:T(8,128)S(1)}, f32[8,128]{1,0:T(8,128)}, u32[]{:S(2)}) copy-start(f32[8,128]{1,0:T(8,128)} %get-tuple-element.115) | copy-start | bytes 12292
  174.5 4.0 %copy-start.26 = (f32[8,128]{1,0:T(8,128)S(1)}, f32[8,128]{1,0:T(8,128)}, u32[]{:S(2)}) copy-start(f32[8,128]{1,0:T(8,128)} %get-tuple-element.131) | copy-start | bytes 12292
  174.5 4.0 %copy-start.30 = (f32[8,128]{1,0:T(8,128)S(1)}, f32[8,128]{1,0:T(8,128)}, u32[]{:S(2)}) copy-start(f32[8,128]{1,0:T(8,128)} %get-tuple-element.125) | copy-start | bytes 12292
  174.5 4.0 %copy-start.31 = (f32[8,128]{1,0:T(8,128)S(1)}, f32[8,128]{1,0:T(8,128)}, u32[]{:S(2)}) copy-start(f32[8,128]{1,0:T(8,128)} %get-tuple-element.123) | copy-start | bytes 12292
  174.5 4.0 %copy-start.33 = (f32[8,128]{1,0:T(8,128)S(1)}, f32[8,128]{1,0:T(8,128)}, u32[]{:S(2)}) copy-start(f32[8,128]{1,0:T(8,128)} %get-tuple-element.121) | copy-start | bytes 12292
  176.0 2.9 %copy-start.25 = (f32[8,128]{1,0:T(8,128)S(1)}, f32[8,128]{1,0:T(8,128)}, u32[]{:S(2)}) copy-start(f32[8,128]{1,0:T(8,128)} %get-tuple-element.95) | copy-start | bytes 12292
  176.0 2.9 %copy-start.27 = (f32[8,128]{1,0:T(8,128)S(1)}, f32[8,128]{1,0:T(8,128)}, u32[]{:S(2)}) copy-start(f32[8,128]{1,0:T(8,128)} %get-tuple-element.89) | copy-start | bytes 12292
  176.0 2.9 %copy-start.28 = (f32[8,128]{1,0:T(8,128)S(1)}, f32[8,128]{1,0:T(8,128)}, u32[]{:S(2)}) copy-start(f32[8,128]{1,0:T(8,128)} %get-tuple-element.87) | copy-start | bytes 12292
  176.0 2.9 %copy-start.29 = (f32[8,128]{1,0:T(8,128)S(1)}, f32[8,128]{1,0:T(8,128)}, u32[]{:S(2)}) copy-start(f32[8,128]{1,0:T(8,128)} %get-tuple-element.85) | copy-start | bytes 12292
  176.4 3.0 %copy-start.8 = (f32[8,128,128]{1,2,0:T(8,128)S(1)}, f32[8,128,128]{1,2,0:T(8,128)}, u32[]{:S(2)}) copy-start(f32[8,128,128]{1,2,0:T(8,128)} %get-tuple-element.114) | copy-start | bytes 1572868
  176.4 3.0 %copy-start.9 = (f32[8,128,128]{1,2,0:T(8,128)S(1)}, f32[8,128,128]{1,2,0:T(8,128)}, u32[]{:S(2)}) copy-start(f32[8,128,128]{1,2,0:T(8,128)} %get-tuple-element.102) | copy-start | bytes 1572868
  (18 other events, 28.4 us)
Sparse Core Ops, SparseCore 0:
  11.6 81.5 all-gather.4
  95.2 72.3 all-gather.2
